TPU v7x, 128 devices: a whole 4x4x4 slice. The times are simulated.
128 devices in a mesh: row: 8 (over z, core), col: 16 (over x, y).
Axes of the slice: x: 4, y: 4, z: 4, core: 2. Of those that a mesh axis runs over, the one named last changes fastest.
Arguments:
- tokens: bfloat16 [2048, 4096], P('row', 'col'), may hold values from -6 to 6
- lengths: int32 [64], P('col'), may hold values from 1 to 64, as said below
- adapter_ids: int32 [64], P('col'), may hold values from 0 to 255, as said below
- adapter_place: int32 [256], replicated, may hold values from 0 to 255, as said below
- attention_qkv_weight: bfloat16 [2048, 6144], P('col', 'row'), may hold values from -0.125 to 0.125
- attention_out_weight: bfloat16 [2048, 2048], P('col', 'row'), may hold values from -0.125 to 0.125
- widen_weight: bfloat16 [2048, 8192], P('col', 'row'), may hold values from -0.125 to 0.125
- contract_weight: bfloat16 [2048, 8192], P('col', 'row'), may hold values from -0.0625 to 0.0625
- first_gain: float32 [2048], P('row'), may hold values from 0.5 to 1.5
- first_shift: float32 [2048], replicated, may hold values from -3 to 3
- second_gain: float32 [2048], replicated, may hold values from 0.5 to 1.5
- second_shift: float32 [2048], replicated, may hold values from -3 to 3
- attend_shrink: bfloat16 [256, 192, 2048], P('col', None, 'row'), may hold values from -0.125 to 0.125
- attend_expand: bfloat16 [256, 3, 64, 2048], P('col', None, None, 'row'), may hold values from -0.75 to 0.75
- output_shrink: bfloat16 [256, 64, 2048], P('col', None, 'row'), may hold values from -0.125 to 0.125
- output_expand: bfloat16 [256, 64, 2048], P('col', None, 'row'), may hold values from -0.75 to 0.75
- upward_shrink: bfloat16 [256, 64, 2048], P('col', None, 'row'), may hold values from -0.125 to 0.125
- upward_expand: bfloat16 [256, 64, 8192], P('col', None, 'row'), may hold values from -0.75 to 0.75
- downward_shrink: bfloat16 [256, 64, 8192], P('col', None, 'row'), may hold values from -0.0625 to 0.0625
- downward_expand: bfloat16 [256, 64, 2048], P('col', None, 'row'), may hold values from -0.75 to 0.75
Outputs:
- layer_out: bfloat16 [2048, 4096], P(None, 'col')
Inputs may be any that keep to these rules, and one draw needn't show every extreme that they name: `lengths`: each aligned block of 4 requests holds a prompt of exactly 64 tokens. `adapter_ids`: in each aligned block of 4 requests, at most 2 name adapters whose store positions lie in one aligned block of 16 positions, and exactly 2 do for some such block. `adapter_place`: A permutation.
All inputs are finite; a program needn't handle non-finite values.
Results may differ from a plain program's by a relative error of at most 0.024.
Values may be sent and summed in bfloat16 or wider, within the bound.
A program may use at most 128 MiB of HBM per device.

v0:
```python
import math
import jax
import jax.numpy as jnp
from jax import lax
from jax.sharding import PartitionSpec as P

D = 2048
HD = 128
CAP = 2
eps = 1e-12
lowrank_scale = 0.5


def fold_weight(shard, combine, initial):
    return combine(initial, lax.all_gather(shard, "col", axis=0, tiled=True), jnp.int32(0))


def project(shard, full_rows):
    initial = jnp.zeros((shard.shape[1], full_rows.shape[1]), jnp.float32)

    def accumulate(total, piece, start):
        return lax.dot_general(
            piece, full_rows, (((0,), (0,)), ((), ())), preferred_element_type=jnp.float32
        )

    return fold_weight(shard, accumulate, initial)


def gather_rows(shard):
    return lax.all_gather(shard, "row", axis=0, tiled=True)


def row_total(value):
    return lax.psum(value.astype(jnp.bfloat16), "row").astype(jnp.float32)


def route_tables(adapter_ids, adapter_place, stored, columns, capacity):
    total_adapters = adapter_place.shape[0]
    match = adapter_ids[:, None] == jnp.arange(total_adapters, dtype=jnp.int32)[None, :]
    position = jnp.sum(jnp.where(match, adapter_place[None, :], 0), axis=1)
    owner = position // stored
    local = position % stored
    count = adapter_ids.shape[0]
    earlier = jnp.arange(count)[None, :] < jnp.arange(count)[:, None]
    same_owner = owner[None, :] == owner[:, None]
    rank = jnp.sum(jnp.where(earlier & same_owner, 1, 0), axis=1).astype(jnp.int32)
    select = (owner[None, None, :] == jnp.arange(columns, dtype=jnp.int32)[:, None, None]) & (
        rank[None, None, :] == jnp.arange(capacity, dtype=jnp.int32)[None, :, None]
    )
    slot_ids = jnp.sum(jnp.where(select, local[None, None, :] + 1, 0), axis=2) - 1
    return (select.astype(jnp.bfloat16), slot_ids)


def expanded_base(expand, reduced):
    return jnp.einsum("ockp,ocks->opcs", expand, reduced, preferred_element_type=jnp.float32)


def expanded_combined(expand, reduced):
    columns, capacity, three, rank, width = expand.shape
    slot = reduced.shape[3]
    grouped = reduced.reshape(columns, capacity, three, rank, slot)
    part = jnp.einsum("ocjkp,ocjks->ojpcs", expand, grouped, preferred_element_type=jnp.float32)
    part = part.reshape(columns, three, width // HD, HD, capacity, slot)
    part = part.transpose(0, 2, 1, 3, 4, 5)
    return part.reshape(columns, three * width, capacity, slot)


def pack_slots(inputs, select):
    columns, capacity, requests = select.shape
    width = inputs.shape[0]
    slot = inputs.shape[1] // requests
    blocks = inputs.reshape(width, requests, slot)
    return jnp.einsum("okj,ijs->oiks", select, blocks, preferred_element_type=jnp.float32).astype(
        jnp.bfloat16
    )


def apply_slots(arrived, shrink, expand, expand_rule):
    partial_result = jnp.einsum(
        "ocki,oics->ocks", shrink, arrived, preferred_element_type=jnp.float32
    )
    reduced = row_total(partial_result).astype(jnp.bfloat16)
    return expand_rule(expand, reduced).astype(jnp.bfloat16)


def unpack_slots(returned, select):
    out_width = returned.shape[1]
    home = jnp.einsum("okj,opks->pjs", select, returned, preferred_element_type=jnp.float32)
    return home.reshape(out_width, -1)


def sent_delta(inputs, select, slot_ids, shrink_store, expand_store, expand_rule):
    packed = pack_slots(inputs, select)
    columns, width, capacity, slot = packed.shape
    arrived, arrived_ids = (
        lax.all_to_all(
            packed.reshape(columns, width, capacity * slot),
            "col",
            split_axis=0,
            concat_axis=0,
            tiled=True,
        ),
        lax.all_to_all(slot_ids, "col", split_axis=0, concat_axis=0, tiled=True),
    )
    arrived = arrived.reshape(columns, width, capacity, slot)
    safe_ids = jnp.maximum(arrived_ids, 0)
    lowrank_update = apply_slots(
        arrived,
        jnp.take(shrink_store, safe_ids, axis=0),
        jnp.take(expand_store, safe_ids, axis=0),
        expand_rule,
    )
    out_width = lowrank_update.shape[1]
    returned = lax.all_to_all(
        lowrank_update.reshape(columns, out_width, capacity * slot),
        "col",
        split_axis=0,
        concat_axis=0,
        tiled=True,
    )
    return unpack_slots(returned.reshape(columns, out_width, capacity, slot), select)


def layer_norm_shard(values, gain, shift):
    sums = row_total(jnp.stack([jnp.sum(values, axis=0), jnp.sum(values * values, axis=0)]))
    mean = sums[0] / D
    square_mean = sums[1] / D
    factor = lax.rsqrt(square_mean - mean * mean + eps)
    return (values - mean) * factor * gain[:, None] + shift[:, None]


def shards(
    tokens,
    lengths,
    adapter_ids,
    adapter_place,
    attention_qkv_weight,
    attention_out_weight,
    widen_weight,
    contract_weight,
    first_gain,
    first_shift,
    second_gain,
    second_shift,
    attend_shrink,
    attend_expand,
    output_shrink,
    output_expand,
    upward_shrink,
    upward_expand,
    downward_shrink,
    downward_expand,
):
    columns = lax.axis_size("col")
    stored = attend_shrink.shape[0]
    select, slot_ids = route_tables(adapter_ids, adapter_place, stored, columns, CAP)
    requests = adapter_ids.shape[0]
    width_portion, token_count = tokens.shape
    slot = token_count // requests
    column_offset = lax.axis_index("row") * width_portion
    stores = (
        (attend_shrink, attend_expand),
        (output_shrink, output_expand),
        (upward_shrink, upward_expand),
        (downward_shrink, downward_expand),
    )

    def adapter_contribution(number, inputs, expand_rule):
        return sent_delta(
            inputs, select, slot_ids, stores[number][0], stores[number][1], expand_rule
        )

    full_tokens = gather_rows(tokens)
    combined_parts = project(attention_qkv_weight, full_tokens)
    combined_parts = combined_parts + lowrank_scale * adapter_contribution(
        0, tokens, expanded_combined
    )
    combined_parts = combined_parts.astype(jnp.bfloat16).reshape(-1, 3, HD, requests, slot)
    query = combined_parts[:, 0]
    keys = combined_parts[:, 1]
    values = combined_parts[:, 2]
    scores = jnp.einsum(
        "hdrq,hdrk->hrqk", query, keys, preferred_element_type=jnp.float32
    ) / math.sqrt(HD)
    valid = jnp.arange(slot, dtype=jnp.int32)[None, :] < lengths[:, None]
    weights = jnp.where(valid[None, :, None, :], jnp.exp(scores), 0.0)
    probs = (weights / jnp.sum(weights, axis=3, keepdims=True)).astype(jnp.bfloat16)
    attended_context = jnp.einsum(
        "hdrk,hrqk->hdrq", values, probs, preferred_element_type=jnp.float32
    )
    attended_context = attended_context.astype(jnp.bfloat16).reshape(-1, token_count)
    full_context = gather_rows(attended_context)
    attention_mixed = project(attention_out_weight, full_context)
    attention_mixed = attention_mixed + lowrank_scale * adapter_contribution(
        1, attended_context, expanded_base
    )
    first_residual_input = tokens.astype(jnp.float32) + attention_mixed
    first_norm_output = layer_norm_shard(
        first_residual_input,
        first_gain,
        lax.dynamic_slice_in_dim(first_shift, column_offset, width_portion, 0),
    ).astype(jnp.bfloat16)
    full_first = gather_rows(first_norm_output)
    hidden_units = project(widen_weight, full_first)
    hidden_units = hidden_units + lowrank_scale * adapter_contribution(
        2, first_norm_output, expanded_base
    )
    hidden_units = jax.nn.gelu(hidden_units, approximate=True).astype(jnp.bfloat16)
    initial = jnp.zeros((D, token_count), jnp.float32)

    def place_rows(total, piece, start):
        return jnp.dot(piece, hidden_units, preferred_element_type=jnp.float32)

    partial_result = fold_weight(contract_weight, place_rows, initial)
    downward_update = adapter_contribution(3, hidden_units, expanded_base)
    own_rows = (
        lax.dynamic_slice_in_dim(partial_result, column_offset, width_portion, 0)
        + lowrank_scale * downward_update
    )
    partial_result = lax.dynamic_update_slice_in_dim(partial_result, own_rows, column_offset, 0)
    summed = row_total(partial_result)
    second_residual_input = full_first.astype(jnp.float32) + summed
    mean = jnp.mean(second_residual_input, axis=0)
    square_mean = jnp.mean(second_residual_input * second_residual_input, axis=0)
    factor = lax.rsqrt(square_mean - mean * mean + eps)
    result = (second_residual_input - mean) * factor * second_gain[:, None] + second_shift[:, None]
    return result.astype(jnp.bfloat16)


def solution(mesh):
    return jax.shard_map(
        shards,
        mesh=mesh,
        in_specs=(
            P("row", "col"),
            P("col"),
            P("col"),
            P(),
            P("col", "row"),
            P("col", "row"),
            P("col", "row"),
            P("col", "row"),
            P("row"),
            P(),
            P(),
            P(),
            P("col", None, "row"),
            P("col", None, None, "row"),
            P("col", None, "row"),
            P("col", None, "row"),
            P("col", None, "row"),
            P("col", None, "row"),
            P("col", None, "row"),
            P("col", None, "row"),
        ),
        out_specs=P(None, "col"),
        check_vma=False,
    )
```

profile of v0, /device:TPU:0, one launch (start us, length us, event | category | flops | bytes accessed | tf_op | source)
XLA Modules:
  0.0 916.0 jit_solution(4494370504113886302)
XLA Ops:
  8.6 7.1 all-to-all-start
  31.0 11.9 %all-to-all-done.1 = bf16[16,256,128]{1,2,0:T(8,128)(2,1)S(1)} async-done(((bf16[16,256,128]{1,2,0:T(8,128)(2,1)}), bf16[16,256,128]{1,2,0:T(8,128)(2,1)S(1)}, u32[]{:S(2)}, u32[]{:S(2)}) %all-to-all-start.1) | async-done | bytes 1048608 | tf_op jit(solution)/shard_map/all_to_all | solution.py:96
  57.5 58.0 %all-reduce.6.cloned.1.call-done = bf16[16,2,3,64,64]{3,4,1,2,0:T(8,128)(2,1)} async-done(((bf16[16,2,3,64,64]{3,4,1,2,0:T(8,128)(2,1)}), bf16[16,2,3,64,64]{3,4,1,2,0:T(8,128)(2,1)}) %all-reduce.6.cloned.1.call-update) | async-done | bytes 786448 | tf_op jit(solution)/shard_map/psum | solution.py:34
  126.2 9.3 %copy.256 = bf16[16,3,2,128,2,64]{3,1,2,5,4,0:T(4,128)(2,1)} copy(bf16[16,3,2,128,2,64]{3,2,5,4,1,0:T(2,128)(2,1)} %convert_element_type.122) | data formatting | bytes 6291456 | tf_op jit(solution)/shard_map/convert_element_type | solution.py:83
  135.5 8.9 convert_element_type.124
  144.4 7.5 all-to-all-start.2
  152.6 42.9 %all-to-all-done.2 = bf16[16,768,128]{1,2,0:T(8,128)(2,1)} async-done(((bf16[16,768,128]{1,2,0:T(8,128)(2,1)}), bf16[16,768,128]{1,2,0:T(8,128)(2,1)}, u32[]{:S(2)}, u32[]{:S(2)}) %all-to-all-start.2) | async-done | bytes 3145760 | tf_op jit(solution)/shard_map/all_to_all | solution.py:114
  200.6 20.6 %all-gather.8.cloned.1.call-done = bf16[2048,768]{1,0:T(8,128)(2,1)} async-done(((bf16[128,768]{1,0:T(8,128)(2,1)}), bf16[2048,768]{1,0:T(8,128)(2,1)}) %all-gather.8.cloned.1.call-update) | async-done | bytes 3145744 | tf_op jit(solution)/shard_map/all_gather | solution.py:15
  239.4 15.2 %all-to-all-done.3 = bf16[16,256,128]{1,2,0:T(8,128)(2,1)} async-done(((bf16[16,256,128]{1,2,0:T(8,128)(2,1)}), bf16[16,256,128]{1,2,0:T(8,128)(2,1)}, u32[]{:S(2)}, u32[]{:S(2)}) %all-to-all-start.3) | async-done | bytes 1048608 | tf_op jit(solution)/shard_map/all_to_all | solution.py:96
  260.6 55.9 %all-reduce.8.cloned.1.call-done = bf16[16,2,64,64]{3,2,1,0:T(8,128)(2,1)} async-done(((bf16[16,2,64,64]{3,2,1,0:T(8,128)(2,1)}), bf16[16,2,64,64]{3,2,1,0:T(8,128)(2,1)}) %all-reduce.8.cloned.1.call-update) | async-done | bytes 262160 | tf_op jit(solution)/shard_map/psum | solution.py:34
  326.8 15.3 %all-to-all-done.4 = bf16[16,256,128]{1,2,0:T(8,128)(2,1)S(1)} async-done(((bf16[16,256,128]{1,2,0:T(8,128)(2,1)}), bf16[16,256,128]{1,2,0:T(8,128)(2,1)S(1)}, u32[]{:S(2)}, u32[]{:S(2)}) %all-to-all-start.4) | async-done | bytes 1048608 | tf_op jit(solution)/shard_map/all_to_all | solution.py:114
  342.8 22.0 %all-gather.14.cloned.1.call-done = bf16[2048,256]{1,0:T(8,128)(2,1)} async-done(((bf16[128,256]{1,0:T(8,128)(2,1)}), bf16[2048,256]{1,0:T(8,128)(2,1)}) %all-gather.14.cloned.1.call-update) | async-done | bytes 1048592 | tf_op jit(solution)/shard_map/all_gather | solution.py:15
  364.8 24.4 %all-gather.12.cloned.1.call-done = bf16[2048,256]{0,1:T(8,128)(2,1)} async-done(((bf16[256,256]{0,1:T(8,128)(2,1)}), bf16[2048,256]{0,1:T(8,128)(2,1)}) %all-gather.12.cloned.1.call-update) | async-done | bytes 1048592 | tf_op jit(solution)/shard_map/all_gather | solution.py:30
  391.4 14.4 %psum.44 = bf16[2,256]{1,0:T(2,128)(2,1)S(1)} all-reduce(bf16[2,256]{1,0:T(2,128)(2,1)S(1)} %pad_maximum_fusion), channel_id=1, replica_groups=mesh['row'=8,'col'=16] {'row'}, use_global_device_ids=true, to_apply=%region_8.10 | all-reduce | flops 512 | bytes 2048 | tf_op jit(solution)/shard_map/psum | solution.py:34
  416.6 13.7 %all-to-all-done.5 = bf16[16,256,128]{1,2,0:T(8,128)(2,1)} async-done(((bf16[16,256,128]{1,2,0:T(8,128)(2,1)}), bf16[16,256,128]{1,2,0:T(8,128)(2,1)}, u32[]{:S(2)}, u32[]{:S(2)}) %all-to-all-start.5) | async-done | bytes 1048608 | tf_op jit(solution)/shard_map/all_to_all | solution.py:96
  436.8 55.5 %all-reduce.10.cloned.1.call-done = bf16[16,2,64,64]{3,2,1,0:T(8,128)(2,1)} async-done(((bf16[16,2,64,64]{3,2,1,0:T(8,128)(2,1)}), bf16[16,2,64,64]{3,2,1,0:T(8,128)(2,1)}) %all-reduce.10.cloned.1.call-update) | async-done | bytes 262160 | tf_op jit(solution)/shard_map/psum | solution.py:34
  505.6 56.7 %all-to-all-done.6 = bf16[16,1024,128]{1,2,0:T(8,128)(2,1)} async-done(((bf16[16,1024,128]{1,2,0:T(8,128)(2,1)}), bf16[16,1024,128]{1,2,0:T(8,128)(2,1)}, u32[]{:S(2)}, u32[]{:S(2)}) %all-to-all-start.6) | async-done | bytes 4194336 | tf_op jit(solution)/shard_map/all_to_all | solution.py:114
  567.6 24.0 %all-gather.18.cloned.1.call-done = bf16[2048,1024]{1,0:T(8,128)(2,1)} async-done(((bf16[128,1024]{1,0:T(8,128)(2,1)}), bf16[2048,1024]{1,0:T(8,128)(2,1)}) %all-gather.18.cloned.1.call-update) | async-done | bytes 4194320 | tf_op jit(solution)/shard_map/all_gather | solution.py:15
  591.6 31.3 %all-gather.16.cloned.1.call-done = bf16[2048,256]{0,1:T(8,128)(2,1)} async-done(((bf16[256,256]{0,1:T(8,128)(2,1)}), bf16[2048,256]{0,1:T(8,128)(2,1)}) %all-gather.16.cloned.1.call-update) | async-done | bytes 1048592 | tf_op jit(solution)/shard_map/all_gather | solution.py:30
  632.8 7.0 all-to-all-start.7
  642.7 53.2 %all-to-all-done.7 = bf16[16,1024,128]{1,2,0:T(8,128)(2,1)} async-done(((bf16[16,1024,128]{1,2,0:T(8,128)(2,1)}), bf16[16,1024,128]{1,2,0:T(8,128)(2,1)}, u32[]{:S(2)}, u32[]{:S(2)}) %all-to-all-start.7) | async-done | bytes 4194336 | tf_op jit(solution)/shard_map/all_to_all | solution.py:96
  703.0 68.0 %all-reduce.12.cloned.1.call-done = bf16[16,2,64,64]{3,2,1,0:T(8,128)(2,1)} async-done(((bf16[16,2,64,64]{3,2,1,0:T(8,128)(2,1)}), bf16[16,2,64,64]{3,2,1,0:T(8,128)(2,1)}) %all-reduce.12.cloned.1.call-update) | async-done | bytes 262160 | tf_op jit(solution)/shard_map/psum | solution.py:34
  780.3 48.7 %all-gather.20.cloned.1.call-done = bf16[2048,1024]{1,0:T(8,128)(2,1)} async-done(((bf16[128,1024]{1,0:T(8,128)(2,1)}), bf16[2048,1024]{1,0:T(8,128)(2,1)}) %all-gather.20.cloned.1.call-update) | async-done | bytes 4194320 | tf_op jit(solution)/shard_map/all_gather | solution.py:15
  839.3 62.7 %all-reduce.14.cloned.1.call-done = bf16[2048,256]{0,1:T(8,128)(2,1)} async-done(((bf16[2048,256]{0,1:T(8,128)(2,1)}), bf16[2048,256]{0,1:T(8,128)(2,1)}) %all-reduce.14.cloned.1.call-update) | async-done | bytes 1048592 | tf_op jit(solution)/shard_map/psum | solution.py:34
  (151 shorter events, 167.4 us)
Async XLA Ops:
  6.5 427.4 %copy-start = (bf16[16,64,1024]{2,1,0:T(8,128)(2,1)S(1)}, bf16[16,64,1024]{2,1,0:T(8,128)(2,1)}, u32[]{:S(2)}) copy-start(bf16[16,64,1024]{2,1,0:T(8,128)(2,1)} %param.41) | copy-start | bytes 6291460
  8.6 14.6 %all-to-all-start = ((s32[16,1,2]{2,1,0:T(1,128)}), s32[16,1,2]{2,1,0:T(1,128)S(1)}, u32[]{:S(2)}, u32[]{:S(2)}) async-start(s32[16,1,2]{2,1,0:T(1,128)} %copy.149), calls=%async_computation | async-start | bytes 16384 | tf_op jit(solution)/shard_map/all_to_all | solution.py:103
  23.2 19.7 %all-to-all-start.1 = ((bf16[16,256,128]{1,2,0:T(8,128)(2,1)}), bf16[16,256,128]{1,2,0:T(8,128)(2,1)S(1)}, u32[]{:S(2)}, u32[]{:S(2)}) async-start(bf16[16,256,128]{1,2,0:T(8,128)(2,1)} %copy.154), calls=%async_computation.1 | async-start | bytes 2097152 | tf_op jit(solution)/shard_map/all_to_all | solution.py:96
  26.9 88.7 %all-reduce.6.cloned.1.call-start = ((), (), s32[]{:S(2)}) async-start(), calls=%async_computation.11 | async-start | bytes 3145728 | tf_op jit(solution)/shard_map/psum | solution.py:34
  52.2 148.4 %all-gather.10.cloned.1.call-start = ((), (), s32[]{:S(2)}) async-start(), calls=%async_computation.10 | async-start | bytes 1179648 | tf_op jit(solution)/shard_map/all_gather | solution.py:30
  52.9 168.3 %all-gather.8.cloned.1.call-start = ((), (), s32[]{:S(2)}) async-start(), calls=%async_computation.9 | async-start | bytes 3342336 | tf_op jit(solution)/shard_map/all_gather | solution.py:15
  144.4 51.0 %all-to-all-start.2 = ((bf16[16,768,128]{1,2,0:T(8,128)(2,1)}), bf16[16,768,128]{1,2,0:T(8,128)(2,1)}, u32[]{:S(2)}, u32[]{:S(2)}) async-start(bf16[16,768,128]{1,2,0:T(8,128)(2,1)} %convert_element_type.124), calls=%async_computation.2 | async-start | bytes 6291456 | tf_op jit(solution)/shard_map/all_to_all | solution.py:114
  233.1 21.5 %all-to-all-start.3 = ((bf16[16,256,128]{1,2,0:T(8,128)(2,1)}), bf16[16,256,128]{1,2,0:T(8,128)(2,1)}, u32[]{:S(2)}, u32[]{:S(2)}) async-start(bf16[16,256,128]{1,2,0:T(8,128)(2,1)} %bitcast.27), calls=%async_computation.3 | async-start | bytes 2097152 | tf_op jit(solution)/shard_map/all_to_all | solution.py:96
  237.5 79.0 %all-reduce.8.cloned.1.call-start = ((), (), s32[]{:S(2)}) async-start(), calls=%async_computation.14 | async-start | bytes 1048576 | tf_op jit(solution)/shard_map/psum | solution.py:34
  257.5 107.4 %all-gather.14.cloned.1.call-start = ((), (), s32[]{:S(2)}) async-start(), calls=%async_computation.13 | async-start | bytes 1114112 | tf_op jit(solution)/shard_map/all_gather | solution.py:15
  258.0 131.2 %all-gather.12.cloned.1.call-start = ((), (), s32[]{:S(2)}) async-start(), calls=%async_computation.12 | async-start | bytes 1179648 | tf_op jit(solution)/shard_map/all_gather | solution.py:30
  319.1 86.7 %copy-start.14 = (f32[256]{0:T(256)S(1)}, f32[256]{0:T(256)}, u32[]{:S(2)}) copy-start(f32[256]{0:T(256)} %param.32) | copy-start | bytes 3076
  319.1 23.0 %all-to-all-start.4 = ((bf16[16,256,128]{1,2,0:T(8,128)(2,1)}), bf16[16,256,128]{1,2,0:T(8,128)(2,1)S(1)}, u32[]{:S(2)}, u32[]{:S(2)}) async-start(bf16[16,256,128]{1,2,0:T(8,128)(2,1)} %bitcast.31), calls=%async_computation.4 | async-start | bytes 2097152 | tf_op jit(solution)/shard_map/all_to_all | solution.py:114
  408.1 22.3 %all-to-all-start.5 = ((bf16[16,256,128]{1,2,0:T(8,128)(2,1)}), bf16[16,256,128]{1,2,0:T(8,128)(2,1)}, u32[]{:S(2)}, u32[]{:S(2)}) async-start(bf16[16,256,128]{1,2,0:T(8,128)(2,1)} %bitcast.44), calls=%async_computation.5 | async-start | bytes 2097152 | tf_op jit(solution)/shard_map/all_to_all | solution.py:96
  414.9 77.4 %all-reduce.10.cloned.1.call-start = ((), (), s32[]{:S(2)}) async-start(), calls=%async_computation.17 | async-start | bytes 1048576 | tf_op jit(solution)/shard_map/psum | solution.py:34
  433.2 158.4 %all-gather.18.cloned.1.call-start = ((), (), s32[]{:S(2)}) async-start(), calls=%async_computation.16 | async-start | bytes 4456448 | tf_op jit(solution)/shard_map/all_gather | solution.py:15
  498.0 64.3 %all-to-all-start.6 = ((bf16[16,1024,128]{1,2,0:T(8,128)(2,1)}), bf16[16,1024,128]{1,2,0:T(8,128)(2,1)}, u32[]{:S(2)}, u32[]{:S(2)}) async-start(bf16[16,1024,128]{1,2,0:T(8,128)(2,1)} %bitcast.185), calls=%async_computation.6 | async-start | bytes 8388608 | tf_op jit(solution)/shard_map/all_to_all | solution.py:114
  504.9 118.0 %all-gather.16.cloned.1.call-start = ((), (), s32[]{:S(2)}) async-start(), calls=%async_computation.15 | async-start | bytes 1179648 | tf_op jit(solution)/shard_map/all_gather | solution.py:30
  632.8 63.2 %all-to-all-start.7 = ((bf16[16,1024,128]{1,2,0:T(8,128)(2,1)}), bf16[16,1024,128]{1,2,0:T(8,128)(2,1)}, u32[]{:S(2)}, u32[]{:S(2)}) async-start(bf16[16,1024,128]{1,2,0:T(8,128)(2,1)} %bitcast.186), calls=%async_computation.7 | async-start | bytes 8388608 | tf_op jit(solution)/shard_map/all_to_all | solution.py:96
  639.8 131.2 %all-reduce.12.cloned.1.call-start = ((), (), s32[]{:S(2)}) async-start(), calls=%async_computation.19 | async-start | bytes 1048576 | tf_op jit(solution)/shard_map/psum | solution.py:34
  701.6 127.5 %all-gather.20.cloned.1.call-start = ((), (), s32[]{:S(2)}) async-start(), calls=%async_computation.18 | async-start | bytes 4456448 | tf_op jit(solution)/shard_map/all_gather | solution.py:15
  702.3 126.7 %copy-start.11 = (bf16[1024,256]{0,1:T(8,128)(2,1)S(1)}, bf16[1024,256]{0,1:T(8,128)(2,1)}, u32[]{:S(2)}) copy-start(bf16[1024,256]{0,1:T(8,128)(2,1)} %copy-done.10) | copy-start | bytes 1572868
  773.5 60.6 %all-to-all-start.8 = ((bf16[16,256,128]{1,2,0:T(8,128)(2,1)}), bf16[16,256,128]{1,2,0:T(8,128)(2,1)S(1)}, u32[]{:S(2)}, u32[]{:S(2)}) async-start(bf16[16,256,128]{1,2,0:T(8,128)(2,1)} %bitcast.64), calls=%async_computation.8 | async-start | bytes 2097152 | tf_op jit(solution)/shard_map/all_to_all | solution.py:114
  780.3 121.7 %all-reduce.14.cloned.1.call-start = ((), (), s32[]{:S(2)}) async-start(), calls=%async_computation.20 | async-start | bytes 2097152 | tf_op jit(solution)/shard_map/psum | solution.py:34
  (13 other events, 276.0 us)
Sparse Core Ops, SparseCore 0:
  52.3 63.2 all-reduce.5
  117.3 22.7 all-gather.9
  142.3 78.8 all-gather.7
  257.6 58.9 all-reduce.7
  318.5 46.2 all-gather.13
  366.3 22.8 all-gather.11
  433.3 59.0 all-reduce.9
  494.5 97.0 all-gather.17
  593.3 29.5 all-gather.15
  701.7 69.2 all-reduce.11
  773.1 55.9 all-gather.19
  839.4 62.5 all-reduce.13
where the time goes:
time: 926 us; the launch traced here: 916 us
  waiting for transfers between devices  688 us (74%)
  local copies, waits for them, and re-layouts  71.5 us (8%)
  matrix products  60.5 us (7%)
  starting transfers between devices  58 us (6%)
  blocking collectives  14.4 us (2%)
  between operations  14.3 us (2%)
    psum x5, waiting for transfers between devices, row_total(): return lax.psum(value.astype(jnp.bfloat16), 'row').astype(jnp.float32)  300 us
    all_gather x4, waiting for transfers between devices, fold_weight(): lax.all_gather(shard, 'col', axis=0, tiled=True)  115 us
    all_to_all x4, waiting for transfers between devices, sent_delta(): lax.all_to_all(lowrank_update.reshape(columns, out_width, capacity * slot...  115 us
    all_to_all x4, waiting for transfers between devices, sent_delta(): lax.all_to_all(packed.reshape(columns, width, capacity * slot), 'col', sp...  94.1 us
    all_gather x3, waiting for transfers between devices, gather_rows(): return lax.all_gather(shard, 'row', axis=0, tiled=True)  55.8 us
    all_to_all x4, starting transfers between devices, sent_delta(): lax.all_to_all(lowrank_update.reshape(columns, out_width, capacity * slot...  28.1 us
    convert_element_type x3, local copies, waits for them, and re-layouts, apply_slots(): return expand_rule(expand, reduced).astype(jnp.bfloat16)  23.7 us
    all_to_all x4, starting transfers between devices, sent_delta(): lax.all_to_all(packed.reshape(columns, width, capacity * slot), 'col', sp...  21.9 us
  transfers between devices with their start and end apart: 21, of which 19 were waited for; matrix products, arithmetic and copies ran while one was open for 9% of the time, Pallas kernels for 0%

commit v1 on v0

--- a/solution.py
+++ b/solution.py
@@ -12,7 +12,24 @@
 
 
 def fold_weight(shard, combine, initial):
-    return combine(initial, lax.all_gather(shard, "col", axis=0, tiled=True), jnp.int32(0))
+
+    def counts_match(block_in):
+        dev_count = lax.axis_size("col")
+        windows = [(tick, (tick + 1) % dev_count) for tick in range(dev_count)]
+        chunks = [(tick, (tick - 1) % dev_count) for tick in range(dev_count)]
+        y1, now = ([block_in], [block_in])
+        for _ in range(dev_count // 2):
+            e_next = lax.ppermute(y1[-1], "col", windows)
+            y1.append(e_next)
+        pp = 0
+        while pp < (dev_count - 1) // 2:
+            x_new = lax.ppermute(now[-1], "col", chunks)
+            now.append(x_new)
+            pp += 1
+        low = jnp.concatenate([*y1[::-1], *now[1:]], axis=0)
+        return jnp.roll(low, (lax.axis_index("col") - dev_count // 2) * block_in.shape[0], axis=0)
+
+    return combine(initial, counts_match(shard), jnp.int32(0))
 
 
 def project(shard, full_rows):

time: 926 us -> 968 us (1.045)
  waiting for transfers between devices: 688 us -> 447 us
  starting transfers between devices: 58 us -> 208 us
  local copies, waits for them, and re-layouts: 71.5 us -> 195 us
    ppermute x0 -> x60, waiting for transfers between devices: none -> 179 us  [the longest x32 172 us: counts_match(): e_next = lax.ppermute(y1[-1], 'col', windows)]
    ppermute x0 -> x60, starting transfers between devices: none -> 150 us  [the longest x28 139 us: counts_match(): x_new = lax.ppermute(now[-1], 'col', chunks)]
    all_gather x4 -> x0, waiting for transfers between devices: 115 us -> none  [fold_weight(): lax.all_gather(shard, 'col', axis=0, tiled=True)]
    unnamed x38 -> x211, local copies, waits for them, and re-layouts: 5.59 us -> 117 us
    all_to_all x4, waiting for transfers between devices: 115 us -> 5.99 us  [sent_delta(): lax.all_to_all(lowrank_update.reshape(columns, out_width, capacity * slot...]
    psum x5, waiting for transfers between devices: 300 us -> 229 us  [row_total(): return lax.psum(value.astype(jnp.bfloat16), 'row').astype(jnp.float32)]
    all_to_all x4, waiting for transfers between devices: 94.1 us -> 24.4 us  [sent_delta(): lax.all_to_all(packed.reshape(columns, width, capacity * slot), 'col', sp...]
    all_gather x3, waiting for transfers between devices: 55.8 us -> 4 us  [gather_rows(): return lax.all_gather(shard, 'row', axis=0, tiled=True)]
  transfers between devices with their start and end apart: 21 -> 77, of which waited for: 19 -> 41; matrix products, arithmetic and copies ran while one was open for 9% -> 24% of each run, Pallas kernels for 0% -> 0%
where the time goes in v1:
time: 968 us; the launch traced here: 956 us
  waiting for transfers between devices  447 us (46%)
  starting transfers between devices  208 us (21%)
  local copies, waits for them, and re-layouts  195 us (20%)
  matrix products  65.7 us (7%)
  blocking collectives  15.6 us (2%)
  between operations  14.7 us (2%)
  other arithmetic  9.91 us (1%)
    psum x5, waiting for transfers between devices, row_total(): return lax.psum(value.astype(jnp.bfloat16), 'row').astype(jnp.float32)  229 us
    ppermute x32, waiting for transfers between devices, counts_match(): e_next = lax.ppermute(y1[-1], 'col', windows)  172 us
    ppermute x28, starting transfers between devices, counts_match(): x_new = lax.ppermute(now[-1], 'col', chunks)  139 us
    unnamed x211, local copies, waits for them, and re-layouts  117 us
    all_to_all x4, starting transfers between devices, sent_delta(): lax.all_to_all(lowrank_update.reshape(columns, out_width, capacity * slot...  27.7 us
    all_to_all x4, waiting for transfers between devices, sent_delta(): lax.all_to_all(packed.reshape(columns, width, capacity * slot), 'col', sp...  24.4 us
    convert_element_type x3, local copies, waits for them, and re-layouts, apply_slots(): return expand_rule(expand, reduced).astype(jnp.bfloat16)  23.6 us
    all_to_all x4, starting transfers between devices, sent_delta(): lax.all_to_all(packed.reshape(columns, width, capacity * slot), 'col', sp...  22.4 us
  transfers between devices with their start and end apart: 77, of which 41 were waited for; matrix products, arithmetic and copies ran while one was open for 24% of the time, Pallas kernels for 0%

profile of v1, /device:TPU:0, one launch (start us, length us, event | category | flops | bytes accessed | tf_op | source)
XLA Modules:
  0.0 955.6 jit_solution(4823535391511917481)
XLA Ops:
  8.6 7.1 all-to-all-start
  33.9 9.2 all-to-all-done.1
  87.1 5.9 collective-permute-start.12
  135.5 5.8 collective-permute-start.27
  153.8 5.9 collective-permute-start.29
  170.3 9.2 copy.265
  179.5 8.9 convert_element_type.124
  188.5 7.2 all-to-all-start.2
  263.9 7.4 all-to-all-start.3
  294.5 55.2 %all-reduce.8.cloned.1.call-done = bf16[16,2,64,64]{3,2,1,0:T(8,128)(2,1)} async-done(((bf16[16,2,64,64]{3,2,1,0:T(8,128)(2,1)}), bf16[16,2,64,64]{3,2,1,0:T(8,128)(2,1)}) %all-reduce.8.cloned.1.call-update) | async-done | bytes 262160 | tf_op jit(solution)/shard_map/psum | solution.py:51
  352.2 6.8 all-to-all-start.4
  377.1 15.6 %psum.44 = bf16[2,256]{1,0:T(2,128)(2,1)S(1)} all-reduce(bf16[2,256]{1,0:T(2,128)(2,1)S(1)} %pad_maximum_fusion), channel_id=1, replica_groups=mesh['row'=8,'col'=16] {'row'}, use_global_device_ids=true, to_apply=%region_8.10 | all-reduce | flops 512 | bytes 2048 | tf_op jit(solution)/shard_map/psum | solution.py:51
  402.0 13.8 %all-to-all-done.5 = bf16[16,256,128]{1,2,0:T(8,128)(2,1)} async-done(((bf16[16,256,128]{1,2,0:T(8,128)(2,1)}), bf16[16,256,128]{1,2,0:T(8,128)(2,1)}, u32[]{:S(2)}, u32[]{:S(2)}) %all-to-all-start.5) | async-done | bytes 1048608 | tf_op jit(solution)/shard_map/all_to_all | solution.py:113
  422.2 55.5 %all-reduce.10.cloned.1.call-done = bf16[16,2,64,64]{3,2,1,0:T(8,128)(2,1)} async-done(((bf16[16,2,64,64]{3,2,1,0:T(8,128)(2,1)}), bf16[16,2,64,64]{3,2,1,0:T(8,128)(2,1)}) %all-reduce.10.cloned.1.call-update) | async-done | bytes 262160 | tf_op jit(solution)/shard_map/psum | solution.py:51
  483.4 6.9 all-to-all-start.6
  495.8 50.1 %collective-permute-done.46 = bf16[128,1024]{1,0:T(8,128)(2,1)S(1)} collective-permute-done((bf16[128,1024]{1,0:T(8,128)(2,1)S(1)}, bf16[128,1024]{1,0:T(8,128)(2,1)S(1)}, u32[]{:S(2)}, u32[]{:S(2)}) %collective-permute-start.46) | collective-permute-done | bytes 262176 | tf_op jit(solution)/shard_map/ppermute | solution.py:22
  581.4 6.5 collective-permute-done.50
  593.2 6.6 collective-permute-done.51
  641.4 7.0 all-to-all-start.7
  650.4 57.3 %collective-permute-done.30 = bf16[128,1024]{1,0:T(8,128)(2,1)S(1)} collective-permute-done((bf16[128,1024]{1,0:T(8,128)(2,1)S(1)}, bf16[128,1024]{1,0:T(8,128)(2,1)S(1)}, u32[]{:S(2)}, u32[]{:S(2)}) %collective-permute-start.30) | collective-permute-done | bytes 262176 | tf_op jit(solution)/shard_map/ppermute | solution.py:22
  758.4 5.9 collective-permute-start.43
  795.7 56.0 %all-reduce.12.cloned.1.call-done = bf16[16,2,64,64]{3,2,1,0:T(8,128)(2,1)} async-done(((bf16[16,2,64,64]{3,2,1,0:T(8,128)(2,1)}), bf16[16,2,64,64]{3,2,1,0:T(8,128)(2,1)}) %all-reduce.12.cloned.1.call-update) | async-done | bytes 262160 | tf_op jit(solution)/shard_map/psum | solution.py:51
  854.2 6.9 all-to-all-start.8
  879.6 61.9 %all-reduce.14.cloned.1.call-done = bf16[2048,256]{0,1:T(8,128)(2,1)} async-done(((bf16[2048,256]{0,1:T(8,128)(2,1)}), bf16[2048,256]{0,1:T(8,128)(2,1)}) %all-reduce.14.cloned.1.call-update) | async-done | bytes 1048592 | tf_op jit(solution)/shard_map/psum | solution.py:51
  (435 shorter events, 462.2 us)
Async XLA Ops:
  27.0 132.7 %all-reduce.6.cloned.1.call-start = ((), (), s32[]{:S(2)}) async-start(), calls=%async_computation.10 | async-start | bytes 3145728 | tf_op jit(solution)/shard_map/psum | solution.py:51
  27.1 26.6 %collective-permute-start = (bf16[128,256]{1,0:T(8,128)(2,1)S(1)}, bf16[128,256]{1,0:T(8,128)(2,1)}, u32[]{:S(2)}, u32[]{:S(2)}) collective-permute-start(bf16[128,256]{1,0:T(8,128)(2,1)S(1)} %copy-done.43), channel_id=1, source_target_pairs={{0,1},{1,2},{2,3},{3,4},{4,5},{5,6},{6,7},{7,8},{8,9},{9,10},{10,1... | collective-permute-start | bytes 196616 | tf_op jit(solution)/shard_map/ppermute | solution.py:22
  52.3 191.3 %all-gather.4.cloned.1.call-start = ((), (), s32[]{:S(2)}) async-start(), calls=%async_computation.9 | async-start | bytes 1179648 | tf_op jit(solution)/shard_map/all_gather | solution.py:47
  52.4 22.8 %collective-permute-start.15 = (bf16[128,768]{1,0:T(8,128)(2,1)S(1)}, bf16[128,768]{1,0:T(8,128)(2,1)S(1)}, u32[]{:S(2)}, u32[]{:S(2)}) collective-permute-start(bf16[128,768]{1,0:T(8,128)(2,1)S(1)} %copy-done.8), channel_id=1, source_target_pairs={{0,1},{1,2},{2,3},{3,4},{4,5},{5,6},{6,7},{7,8},{8,9},{9,10},{10,1... | collective-permute-start | bytes 589832 | tf_op jit(solution)/shard_map/ppermute | solution.py:22
  69.7 24.3 %collective-permute-start.23 = (bf16[128,768]{1,0:T(8,128)(2,1)S(1)}, bf16[128,768]{1,0:T(8,128)(2,1)}, u32[]{:S(2)}, u32[]{:S(2)}) collective-permute-start(bf16[128,768]{1,0:T(8,128)(2,1)S(1)} %copy-done.8), channel_id=1, source_target_pairs={{0,15},{1,0},{2,1},{3,2},{4,3},{5,4},{6,5},{7,6},{8,7},{9,8},{10,9... | collective-permute-start | bytes 589832 | tf_op jit(solution)/shard_map/ppermute | solution.py:26
  75.2 26.1 %collective-permute-start.16 = (bf16[128,768]{1,0:T(8,128)(2,1)S(1)}, bf16[128,768]{1,0:T(8,128)(2,1)}, u32[]{:S(2)}, u32[]{:S(2)}) collective-permute-start(bf16[128,768]{1,0:T(8,128)(2,1)S(1)} %collective-permute-done.15), channel_id=1, source_target_pairs={{0,1},{1,2},{2,3},{3,4},{4,5},{5,6},{6,7},{7,8},{8,9},{9,10},{10,1... | collective-permute-start | bytes 589832 | tf_op jit(solution)/shard_map/ppermute | solution.py:22
  118.0 160.4 %collective-permute-start.14 = (bf16[128,256]{1,0:T(8,128)(2,1)}, bf16[128,256]{1,0:T(8,128)(2,1)}, u32[]{:S(2)}, u32[]{:S(2)}) collective-permute-start(bf16[128,256]{1,0:T(8,128)(2,1)} %collective-permute-done.13), channel_id=1, source_target_pairs={{0,15},{1,0},{2,1},{3,2},{4,3},{5,4},{6,5},{7,6},{8,7},{9,8},{10,9... | collective-permute-start | bytes 196616 | tf_op jit(solution)/shard_map/ppermute | solution.py:26
  153.8 62.7 %collective-permute-start.29 = (bf16[128,768]{1,0:T(8,128)(2,1)}, bf16[128,768]{1,0:T(8,128)(2,1)}, u32[]{:S(2)}, u32[]{:S(2)}) collective-permute-start(bf16[128,768]{1,0:T(8,128)(2,1)} %collective-permute-done.28), channel_id=1, source_target_pairs={{0,15},{1,0},{2,1},{3,2},{4,3},{5,4},{6,5},{7,6},{8,7},{9,8},{10,9... | collective-permute-start | bytes 589832 | tf_op jit(solution)/shard_map/ppermute | solution.py:26
  159.7 36.0 %collective-permute-start.22 = (bf16[128,768]{1,0:T(8,128)(2,1)}, bf16[128,768]{1,0:T(8,128)(2,1)}, u32[]{:S(2)}, u32[]{:S(2)}) collective-permute-start(bf16[128,768]{1,0:T(8,128)(2,1)} %collective-permute-done.21), channel_id=1, source_target_pairs={{0,1},{1,2},{2,3},{3,4},{4,5},{5,6},{6,7},{7,8},{8,9},{9,10},{10,1... | collective-permute-start | bytes 589832 | tf_op jit(solution)/shard_map/ppermute | solution.py:22
  188.5 48.1 %all-to-all-start.2 = ((bf16[16,768,128]{1,2,0:T(8,128)(2,1)}), bf16[16,768,128]{1,2,0:T(8,128)(2,1)}, u32[]{:S(2)}, u32[]{:S(2)}) async-start(bf16[16,768,128]{1,2,0:T(8,128)(2,1)} %convert_element_type.124), calls=%async_computation.2 | async-start | bytes 6291456 | tf_op jit(solution)/shard_map/all_to_all | solution.py:131
  271.3 78.3 %all-reduce.8.cloned.1.call-start = ((), (), s32[]{:S(2)}) async-start(), calls=%async_computation.12 | async-start | bytes 1048576 | tf_op jit(solution)/shard_map/psum | solution.py:51
  287.1 87.8 %all-gather.6.cloned.1.call-start = ((), (), s32[]{:S(2)}) async-start(), calls=%async_computation.11 | async-start | bytes 1179648 | tf_op jit(solution)/shard_map/all_gather | solution.py:47
  400.2 77.5 %all-reduce.10.cloned.1.call-start = ((), (), s32[]{:S(2)}) async-start(), calls=%async_computation.14 | async-start | bytes 1048576 | tf_op jit(solution)/shard_map/psum | solution.py:51
  418.7 71.6 %collective-permute-start.45 = (bf16[128,1024]{1,0:T(8,128)(2,1)S(1)}, bf16[128,1024]{1,0:T(8,128)(2,1)S(1)}, u32[]{:S(2)}, u32[]{:S(2)}) collective-permute-start(bf16[128,1024]{1,0:T(8,128)(2,1)S(1)} %copy-done.23), channel_id=1, source_target_pairs={{0,1},{1,2},{2,3},{3,4},{4,5},{5,6},{6,7},{7,8},{8,9},{9,10},{10,1... | collective-permute-start | bytes 786440 | tf_op jit(solution)/shard_map/ppermute | solution.py:22
  483.4 137.7 %all-to-all-start.6 = ((bf16[16,1024,128]{1,2,0:T(8,128)(2,1)}), bf16[16,1024,128]{1,2,0:T(8,128)(2,1)}, u32[]{:S(2)}, u32[]{:S(2)}) async-start(bf16[16,1024,128]{1,2,0:T(8,128)(2,1)} %bitcast.164), calls=%async_computation.6 | async-start | bytes 8388608 | tf_op jit(solution)/shard_map/all_to_all | solution.py:131
  490.3 140.2 %all-gather.8.cloned.1.call-start = ((), (), s32[]{:S(2)}) async-start(), calls=%async_computation.13 | async-start | bytes 1179648 | tf_op jit(solution)/shard_map/all_gather | solution.py:47
  490.3 55.6 %collective-permute-start.46 = (bf16[128,1024]{1,0:T(8,128)(2,1)S(1)}, bf16[128,1024]{1,0:T(8,128)(2,1)S(1)}, u32[]{:S(2)}, u32[]{:S(2)}) collective-permute-start(bf16[128,1024]{1,0:T(8,128)(2,1)S(1)} %collective-permute-done.45), channel_id=1, source_target_pairs={{0,1},{1,2},{2,3},{3,4},{4,5},{5,6},{6,7},{7,8},{8,9},{9,10},{10,1... | collective-permute-start | bytes 786440 | tf_op jit(solution)/shard_map/ppermute | solution.py:22
  492.3 53.6 %collective-permute-start.53 = (bf16[128,1024]{1,0:T(8,128)(2,1)S(1)}, bf16[128,1024]{1,0:T(8,128)(2,1)S(1)}, u32[]{:S(2)}, u32[]{:S(2)}) collective-permute-start(bf16[128,1024]{1,0:T(8,128)(2,1)S(1)} %copy-done.23), channel_id=1, source_target_pairs={{0,15},{1,0},{2,1},{3,2},{4,3},{5,4},{6,5},{7,6},{8,7},{9,8},{10,9... | collective-permute-start | bytes 786440 | tf_op jit(solution)/shard_map/ppermute | solution.py:26
  641.4 147.3 %all-to-all-start.7 = ((bf16[16,1024,128]{1,2,0:T(8,128)(2,1)}), bf16[16,1024,128]{1,2,0:T(8,128)(2,1)}, u32[]{:S(2)}, u32[]{:S(2)}) async-start(bf16[16,1024,128]{1,2,0:T(8,128)(2,1)} %bitcast.165), calls=%async_computation.7 | async-start | bytes 8388608 | tf_op jit(solution)/shard_map/all_to_all | solution.py:113
  648.4 203.3 %all-reduce.12.cloned.1.call-start = ((), (), s32[]{:S(2)}) async-start(), calls=%async_computation.15 | async-start | bytes 1048576 | tf_op jit(solution)/shard_map/psum | solution.py:51
  648.4 59.2 %collective-permute-start.30 = (bf16[128,1024]{1,0:T(8,128)(2,1)S(1)}, bf16[128,1024]{1,0:T(8,128)(2,1)S(1)}, u32[]{:S(2)}, u32[]{:S(2)}) collective-permute-start(bf16[128,1024]{1,0:T(8,128)(2,1)S(1)} %copy-done.24), channel_id=1, source_target_pairs={{0,1},{1,2},{2,3},{3,4},{4,5},{5,6},{6,7},{7,8},{8,9},{9,10},{10,1... | collective-permute-start | bytes 786440 | tf_op jit(solution)/shard_map/ppermute | solution.py:22
  771.8 94.1 %collective-permute-start.44 = (bf16[128,1024]{1,0:T(8,128)(2,1)}, bf16[128,1024]{1,0:T(8,128)(2,1)}, u32[]{:S(2)}, u32[]{:S(2)}) collective-permute-start(bf16[128,1024]{1,0:T(8,128)(2,1)} %collective-permute-done.43), channel_id=1, source_target_pairs={{0,15},{1,0},{2,1},{3,2},{4,3},{5,4},{6,5},{7,6},{8,7},{9,8},{10,9... | collective-permute-start | bytes 786440 | tf_op jit(solution)/shard_map/ppermute | solution.py:26
  854.2 22.1 %all-to-all-start.8 = ((bf16[16,256,128]{1,2,0:T(8,128)(2,1)}), bf16[16,256,128]{1,2,0:T(8,128)(2,1)}, u32[]{:S(2)}, u32[]{:S(2)}) async-start(bf16[16,256,128]{1,2,0:T(8,128)(2,1)} %bitcast.60), calls=%async_computation.8 | async-start | bytes 2097152 | tf_op jit(solution)/shard_map/all_to_all | solution.py:131
  861.1 80.4 %all-reduce.14.cloned.1.call-start = ((), (), s32[]{:S(2)}) async-start(), calls=%async_computation.16 | async-start | bytes 2097152 | tf_op jit(solution)/shard_map/psum | solution.py:51
  (110 other events, 2606.5 us)
Sparse Core Ops, SparseCore 0:
  52.4 64.0 all-reduce.5
  118.3 22.4 all-gather.3
  287.2 62.3 all-reduce.7
  351.2 22.4 all-gather.5
  418.8 58.8 all-reduce.9
  611.9 18.5 all-gather.7
  794.4 57.2 all-reduce.11
  879.7 61.7 all-reduce.13
